TPU v7x, 32 devices: a whole 2x2x4 slice. The times are simulated.
32 devices in a mesh: param: 4 (over y, core), ex: 8 (over z, x).
Axes of the slice: x: 2, y: 2, z: 4, core: 2. Of those that a mesh axis runs over, the one named last changes fastest.
Arguments:
- activations: bfloat16 [512, 128, 8192], P('ex', None, 'param'), may hold values from -8 to 8
- cotangents: bfloat16 [512, 128, 64], P('ex'), may hold values from -8 to 8
- token_ids: int32 [512, 128], P('ex'), may hold values from 0 to 128255, as said below
- signs: int32 [64, 8192], P(None, 'param'), may hold values from -1 to 1, as said below
- select: int32 [32768], replicated, may hold values from 0 to 524287, as said below
Outputs:
- features: float32 [512, 32768], P('ex', 'param')
- gram: float32 [512, 512], P('ex')
Inputs may be any that keep to these rules, and one draw needn't show every extreme that they name: `token_ids`: in each example the nonzero ids come first and zeros fill the rest; at least 32 positions of every example are nonzero. `signs`: every entry is 1 or -1. `select`: the 32768 entries are distinct.
All inputs are finite; a program needn't handle non-finite values.
Results may differ from a plain program's by a relative error of at most 0.0003.
Values sent between devices are 32-bit elements; how exact they have to be, the bound alone decides.
A program may use at most 192 MiB of HBM per device.

v0:
```python
import math

import jax
import jax.numpy as jnp
from jax import lax
from jax.sharding import PartitionSpec as P

D = 8192
SLAB = 64
TOKS = 128
K = 32768


def walsh_table(table_order):
    row_index = lax.broadcasted_iota(jnp.int32, (table_order, table_order), 0)
    column_index = lax.broadcasted_iota(jnp.int32, (table_order, table_order), 1)
    common_bits = row_index & column_index
    parity = jnp.zeros((table_order, table_order), jnp.int32)
    for bit_index in range(table_order.bit_length() - 1):
        parity = parity ^ common_bits >> bit_index & 1
    return (1 - 2 * parity).astype(jnp.float32)


def body(activations, cotangents, token_ids, signs, select):
    highest = lax.Precision.HIGHEST
    count_ex = activations.shape[0]
    local_width = activations.shape[2]
    slab_rows = cotangents.shape[2]
    live_mask = token_ids != 0
    masked = jnp.where(live_mask[:, :, None], cotangents, jnp.zeros((), cotangents.dtype))
    gradient = jnp.einsum(
        "etr,etc->erc", masked, activations, preferred_element_type=jnp.float32
    ) * (1.0 / math.sqrt(TOKS))
    flipped = gradient * signs.astype(jnp.float32)[None, :, :]
    mixed = jnp.einsum("rs,esc->erc", walsh_table(slab_rows), flipped, precision=highest)
    inner_order = min(local_width, 128)
    outer_order = local_width // inner_order
    blocked = mixed.reshape(count_ex, slab_rows, outer_order, inner_order)
    blocked = jnp.einsum("erab,bd->erad", blocked, walsh_table(inner_order), precision=highest)
    blocked = jnp.einsum("erab,ax->erxb", blocked, walsh_table(outer_order), precision=highest)
    local_values = blocked.reshape(count_ex, slab_rows, local_width)
    factor = 1.0 / math.sqrt(SLAB * D)
    my_index = lax.axis_index("param")
    section_count = lax.axis_size("param").bit_length() - 1
    column = select % D
    owner_block = column // local_width
    position = select // D * local_width + column % local_width
    shared = owner_block & my_index
    parity = jnp.zeros_like(shared)
    for bit_index in range(section_count):
        parity = parity ^ shared >> bit_index & 1
    weight = (1 - 2 * parity).astype(jnp.float32) * factor
    partial_term = jnp.take(local_values.reshape(count_ex, -1), position, axis=1) * weight[None, :]
    features = lax.psum_scatter(partial_term, "param", scatter_dimension=1, tiled=True)
    tile_block = jnp.einsum(
        "ek,fk->ef", features, lax.all_gather(features, "ex", axis=0, tiled=True), precision=highest
    )
    gram = lax.psum(tile_block, "param") / K
    return (features, gram)


def solution(mesh):
    return jax.shard_map(
        body,
        mesh=mesh,
        in_specs=(
            P("ex", None, "param"),
            P("ex", None, None),
            P("ex", None),
            P(None, "param"),
            P(),
        ),
        out_specs=(P("ex", "param"), P("ex", None)),
        check_vma=False,
    )
```

profile of v0, /device:TPU:0, one launch (start us, length us, event | category | flops | bytes accessed | tf_op | source)
XLA Modules:
  0.0 1108.2 jit_solution(2476731993091262934)
XLA Ops:
  7.2 0.0 reduce-scatter.2.cloned.1.call-start
  7.2 0.8 broadcast_compare_fusion
  8.0 1.1 convert_multiply_fusion
  9.1 21.6 %fusion.5 = f32[64,64,2048]{2,1,0:T(8,128)} fusion(bf16[64,128,2048]{2,1,0:T(8,128)(2,1)} %param.5, bf16[64,128,64]{1,2,0:T(8,128)(2,1)} %param.6, pred[64,128]{1,0:T(8,128)(4,1)S(1)} %broadcast_compare_fusion), kind=kOutput, calls=%fused_computation.8 | convolution fusion | flops 2148007936 | bytes 68165632 | tf_op jit(solution)/shard_map/etr,etc->erc/dot_general | solution.py:31
  30.7 44.3 %fusion.2 = f32[64,2048,64]{1,2,0:T(8,128)} fusion(f32[64,64,2048]{2,1,0:T(8,128)} %fusion.5, f32[64,2048]{1,0:T(8,128)S(1)} %convert_multiply_fusion), kind=kOutput, calls=%fused_computation.3 | convolution fusion | flops 6450925568 | bytes 67633152 | tf_op jit(solution)/shard_map/rs,esc->erc/dot_general | solution.py:35
  74.9 17.2 %copy.15 = f32[512,8,16,128]{3,2,1,0:T(8,128)S(1)} copy(f32[512,8,16,128]{3,1,2,0:T(8,128)} %bitcast.34) | data formatting | bytes 67108864
  92.2 32.2 %fusion = f32[64,64,16,128]{3,2,1,0:T(8,128)} fusion(f32[64,64,16,128]{3,2,1,0:T(8,128)S(1)} %bitcast.35), kind=kOutput, calls=%fused_computation.1 | convolution fusion | flops 12885295104 | bytes 67108864 | tf_op jit(solution)/shard_map/erab,bd->erad/dot_general | solution.py:39
  124.3 35.9 %convolution_bitcast_fusion = f32[64,64,16,128]{3,2,1,0:T(8,128)} fusion(f32[64,64,16,128]{3,2,1,0:T(8,128)} %fusion), kind=kOutput, calls=%fused_computation.7 | convolution fusion | flops 1610616576 | bytes 67108864 | tf_op jit(solution)/shard_map/erab,ax->erxb/dot_general | solution.py:40
  160.3 45.0 %copy.14 = f32[64,64,16,128]{0,3,2,1:T(8,128)} copy(f32[64,64,16,128]{3,2,1,0:T(8,128)} %convolution_bitcast_fusion) | data formatting | bytes 67108864 | tf_op jit(solution)/shard_map/reshape;reshape | solution.py:53
  205.2 0.2 compare_and_fusion
  205.5 0.2 convert_multiply_fusion.1
  205.7 472.7 %gather_fusion = f32[32768,64]{1,0:T(8,128)} fusion(f32[64,131072]{0,1:T(8,128)} %bitcast.7, s32[32768]{0:T(1024)S(1)} %broadcast_clamp_fusion), kind=kCustom, calls=%fused_computation | custom fusion | bytes 16908288 | tf_op jit(solution)/shard_map/jit(_take)/gather | solution.py:53
  678.4 13.2 %multiply_bitcast_fusion = f32[64,32768]{0,1:T(8,128)} fusion(f32[32768,64]{1,0:T(8,128)} %gather_fusion, f32[32768]{0:T(1024)S(1)} %convert_multiply_fusion.1, pred[32768]{0:T(1024)(128)(4,1)S(1)} %get-tuple-element.6), kind=kLoop, calls=%fused_computation.5 | loop fusion | flops 4194304 | bytes 16941056 | tf_op jit(solution)/shard_map/mul | solution.py:53
  691.6 0.0 reduce-scatter.2.cloned.1.call-update
  691.6 0.0 all-gather.2.cloned.1.call-start
  691.7 127.9 %reduce-scatter.2.cloned.1.call-done = f32[64,8192]{0,1:T(8,128)} async-done(((f32[64,32768]{0,1:T(8,128)}), f32[64,8192]{0,1:T(8,128)}) %reduce-scatter.2.cloned.1.call-update) | async-done | bytes 2097168 | tf_op jit(solution)/shard_map/reduce_scatter | solution.py:54
  819.5 3.8 copy.11
  823.3 0.0 all-gather.2.cloned.1.call-update
  823.4 0.0 all-reduce.2.cloned.1.call-start
  823.4 227.4 %all-gather.2.cloned.1.call-done = f32[512,8192]{1,0:T(8,128)} async-done(((f32[64,8192]{1,0:T(8,128)}), f32[512,8192]{1,0:T(8,128)}) %all-gather.2.cloned.1.call-update) | async-done | bytes 16777232 | tf_op jit(solution)/shard_map/all_gather | solution.py:56
  1050.8 19.1 %fusion.120 = f32[64,512]{1,0:T(8,128)} fusion(f32[64,8192]{0,1:T(8,128)} %reduce-scatter.2.cloned.1.call-done, f32[512,8192]{1,0:T(8,128)} %all-gather.2.cloned.1.call-done), kind=kOutput, calls=%fused_computation.142 | convolution fusion | flops 3221225472 | bytes 19005440 | tf_op jit(solution)/shard_map/ek,fk->ef/dot_general | solution.py:55
  1069.9 0.0 all-reduce.2.cloned.1.call-update
  1069.9 30.1 %all-reduce.2.cloned.1.call-done = f32[64,512]{1,0:T(8,128)} async-done(((f32[64,512]{1,0:T(8,128)}), f32[64,512]{1,0:T(8,128)}) %all-reduce.2.cloned.1.call-update) | async-done | bytes 131088 | tf_op jit(solution)/shard_map/psum | solution.py:58
  1100.1 1.6 broadcast_multiply_fusion
  (3 shorter events, 0.0 us)
Async XLA Ops:
  7.2 812.4 %reduce-scatter.2.cloned.1.call-start = ((), (), s32[]{:S(2)}) async-start(), calls=%async_computation.1 | async-start | bytes 20971520 | tf_op jit(solution)/shard_map/reduce_scatter | solution.py:54
  160.3 45.0 %copy-start = (s32[32768]{0:T(1024)S(1)}, s32[32768]{0:T(1024)}, u32[]{:S(2)}) copy-start(s32[32768]{0:T(1024)} %param.9) | copy-start | bytes 393220
  691.6 359.1 %all-gather.2.cloned.1.call-start = ((), (), s32[]{:S(2)}) async-start(), calls=%async_computation.2 | async-start | bytes 18874368 | tf_op jit(solution)/shard_map/all_gather | solution.py:56
  823.4 276.7 %all-reduce.2.cloned.1.call-start = ((), (), s32[]{:S(2)}) async-start(), calls=%async_computation.3 | async-start | bytes 262144 | tf_op jit(solution)/shard_map/psum | solution.py:58
Sparse Core Ops, SparseCore 0:
  691.8 127.7 reduce-scatter.1
  823.5 227.2 all-gather.1
  1070.1 29.9 all-reduce.1
where the time goes:
time: 1110 us
  local copies, waits for them, and re-layouts  539 us (49%)
  waiting for transfers between devices  385 us (35%)
  matrix products  153 us (14%)
  other arithmetic  17.1 us (2%)
  between operations  13.8 us (1%)
    gather x1, local copies, waits for them, and re-layouts, body(): jnp.take(local_values.reshape(count_ex, -1), position, axis=1)  473 us
    all_gather x1, waiting for transfers between devices, body(): lax.all_gather(features, 'ex', axis=0, tiled=True)  227 us
    reduce_scatter x1, waiting for transfers between devices, body(): lax.psum_scatter(partial_term, 'param', scatter_dimension=1, tiled=True)  128 us
    another operation x1, local copies, waits for them, and re-layouts, body(): local_values.reshape(count_ex, -1)  45 us
    dot_general x1, matrix products, body(): jnp.einsum('rs,esc->erc', walsh_table(slab_rows), flipped, precision=high...  44.3 us
    dot_general x1, matrix products, body(): jnp.einsum('erab,ax->erxb', blocked, walsh_table(outer_order), precision=...  35.9 us
    dot_general x1, matrix products, body(): jnp.einsum('erab,bd->erad', blocked, walsh_table(inner_order), precision=...  32.2 us
    psum x1, waiting for transfers between devices, body(): gram = lax.psum(tile_block, 'param') / K  30.1 us
  transfers between devices with their start and end apart: 3, of which 3 were waited for; matrix products, arithmetic and copies ran while one was open for 0% of the time, Pallas kernels for 0%

commit v1 on v0

v1 whole, which is shorter than its diff:
```python
import functools

import jax
import jax.numpy as jnp
from jax import lax
from jax.experimental import pallas as pl
from jax.experimental.pallas import tpu as pltpu
from jax.sharding import PartitionSpec as P

LANES = 128
GROUP = 8


def walsh_table(table_order):
    row_index = lax.broadcasted_iota(jnp.int32, (table_order, table_order), 0)
    column_index = lax.broadcasted_iota(jnp.int32, (table_order, table_order), 1)
    common_bits = row_index & column_index
    parity = jnp.zeros((table_order, table_order), jnp.int32)
    for bit_index in range(table_order.bit_length() - 1):
        parity = parity ^ common_bits >> bit_index & 1
    return (1 - 2 * parity).astype(jnp.float32)


def split_two(value):
    high = value.astype(jnp.bfloat16)
    low = (value - high.astype(jnp.float32)).astype(jnp.bfloat16)
    return high, low


def mix_kernel(cots_ref, acts_ref, signs_ref, table_ref, out_ref, held):
    slab_rows = out_ref.shape[0]
    blocks = out_ref.shape[2] // LANES
    flip = signs_ref[...].astype(jnp.float32)
    for e in range(GROUP):
        gradient = jnp.dot(cots_ref[e], acts_ref[e], preferred_element_type=jnp.float32)
        high, low = split_two(gradient * flip)
        mixed = jnp.dot(
            table_ref[...], jnp.concatenate([high, low], axis=0), preferred_element_type=jnp.float32
        )
        for c in range(blocks):
            held[pl.ds((c * GROUP + e) * slab_rows, slab_rows), :] = mixed[:, c * LANES:(c + 1) * LANES]
    for r in range(slab_rows):
        for c in range(blocks):
            out_ref[r, :, c * LANES:(c + 1) * LANES] = held[
                pl.ds(c * GROUP * slab_rows + r, GROUP, stride=slab_rows), :
            ]


def mix_rows(cots, acts, signs, table):
    count_ex, slab_rows, toks = cots.shape
    width = acts.shape[2]
    block = min(width, 1024)
    return pl.pallas_call(
        mix_kernel,
        grid=(width // block, count_ex // GROUP),
        in_specs=[
            pl.BlockSpec((GROUP, slab_rows, toks), lambda c, e: (e, 0, 0)),
            pl.BlockSpec((GROUP, toks, block), lambda c, e: (e, 0, c)),
            pl.BlockSpec((slab_rows, block), lambda c, e: (0, c)),
            pl.BlockSpec(table.shape, lambda c, e: (0, 0)),
        ],
        out_specs=pl.BlockSpec((slab_rows, GROUP, block), lambda c, e: (0, e, c)),
        out_shape=jax.ShapeDtypeStruct((slab_rows, count_ex, width), jnp.float32),
        scratch_shapes=[pltpu.VMEM((GROUP * slab_rows * block // LANES, LANES), jnp.float32)],
    )(cots, acts, signs, table)


def pick_kernel(steps, rows_ref, mixed_ref, table_ref, upper_ref, weight_ref, out_ref, values, pieces, picked):
    step = pl.program_id(0)
    count_ex, width = mixed_ref.shape[2], mixed_ref.shape[3]
    blocks = width // LANES
    chunk = out_ref.shape[1]

    @pl.when(step < steps)
    def _():
        for half in range(2):
            for i in range(count_ex // 16):
                part = [
                    mixed_ref[half, 0, i * 16:(i + 1) * 16, a * LANES:(a + 1) * LANES] for a in range(blocks)
                ]
                span = 1
                while span < blocks:
                    part = [
                        part[a] + part[a + span] if a & span == 0 else part[a - span] - part[a]
                        for a in range(blocks)
                    ]
                    span *= 2
                row = half * count_ex + i * 16
                for a in range(blocks):
                    high, low = split_two(part[a])
                    pieces[row:row + 16, 2 * a * LANES:(2 * a + 1) * LANES] = high
                    pieces[row:row + 16, (2 * a + 1) * LANES:(2 * a + 2) * LANES] = low
        base = pl.multiple_of(step * width, LANES)
        for a in range(blocks):
            values[pl.ds(base + a * LANES, LANES), :] = lax.dot_general(
                table_ref[...],
                pieces[:, 2 * a * LANES:(2 * a + 2) * LANES],
                (((1,), (1,)), ((), ())),
                preferred_element_type=jnp.float32,
            )

    @pl.when(step >= steps)
    def _():
        start = (step - steps) * chunk

        def pick(i, carry):
            first = pl.multiple_of(i * 32, 32)
            taken = [values[pl.ds(rows_ref[start + first + j], 1), :] for j in range(32)]
            for j in range(32):
                picked[pl.ds(first + j, 1), :] = taken[j]
            return carry

        lax.fori_loop(0, chunk // 32, pick, 0)
        turned = picked[...].T
        out_ref[...] = jnp.where(upper_ref[...] > 0, turned[count_ex:], turned[:count_ex]) * weight_ref[...]


def pick_features(rows, mixed, table, upper, weight):
    slab_rows, count_ex, width = mixed.shape
    count = rows.shape[0]
    steps = slab_rows // 2
    chunk = min(count, 1024)
    halves = mixed.reshape(2, steps, count_ex, width)
    return pl.pallas_call(
        functools.partial(pick_kernel, steps),
        grid_spec=pltpu.PrefetchScalarGridSpec(
            num_scalar_prefetch=1,
            grid=(steps + count // chunk,),
            in_specs=[
                pl.BlockSpec((2, 1, count_ex, width), lambda s, rows: (0, jnp.minimum(s, steps - 1), 0, 0)),
                pl.BlockSpec(table.shape, lambda s, rows: (0, 0)),
                pl.BlockSpec((1, chunk), lambda s, rows: (0, jnp.maximum(s - steps, 0))),
                pl.BlockSpec((1, chunk), lambda s, rows: (0, jnp.maximum(s - steps, 0))),
            ],
            out_specs=pl.BlockSpec((count_ex, chunk), lambda s, rows: (0, jnp.maximum(s - steps, 0))),
            scratch_shapes=[
                pltpu.VMEM((steps * width, LANES), jnp.float32),
                pltpu.VMEM((2 * count_ex, 2 * width), jnp.bfloat16),
                pltpu.VMEM((chunk, LANES), jnp.float32),
            ],
        ),
        out_shape=jax.ShapeDtypeStruct((count_ex, count), jnp.float32),
        compiler_params=pltpu.CompilerParams(vmem_limit_bytes=60 * 1024 * 1024),
    )(rows, halves, table, upper, weight)


def body(activations, cotangents, token_ids, signs, select):
    local_width = activations.shape[2]
    toks = activations.shape[1]
    slab_rows = cotangents.shape[2]
    section_count = lax.axis_size("param")
    width = local_width * section_count
    live_mask = token_ids != 0
    masked = jnp.where(live_mask[:, :, None], cotangents, jnp.zeros((), cotangents.dtype))
    row_table = walsh_table(slab_rows).astype(jnp.bfloat16)
    lane_table = walsh_table(LANES).astype(jnp.bfloat16)
    mixed = mix_rows(
        jnp.swapaxes(masked, 1, 2), activations, signs, jnp.concatenate([row_table, row_table], axis=1)
    )
    factor = 1.0 / float(toks * slab_rows * width) ** 0.5
    my_index = lax.axis_index("param")
    column = select % width
    row = select // width
    shared = column // local_width & my_index
    parity = jnp.zeros_like(shared)
    for bit_index in range(section_count.bit_length() - 1):
        parity = parity ^ shared >> bit_index & 1
    weight = (1 - 2 * parity).astype(jnp.float32) * factor
    half_rows = slab_rows // 2
    rows = row % half_rows * local_width + column % local_width
    upper = (row // half_rows).astype(jnp.float32)
    partial_term = pick_features(
        rows, mixed, jnp.concatenate([lane_table, lane_table], axis=1), upper[None, :], weight[None, :]
    )
    features = lax.psum_scatter(partial_term, "param", scatter_dimension=1, tiled=True)
    swapped = lax.all_to_all(features, "ex", split_axis=1, concat_axis=0, tiled=True)
    tile = lax.dot_general(
        swapped, swapped, (((1,), (1,)), ((), ())), precision=lax.Precision.HIGHEST
    )
    tile_block = lax.psum_scatter(tile, "ex", scatter_dimension=0, tiled=True)
    gram = lax.psum(tile_block, "param") / select.shape[0]
    return (features, gram)


def solution(mesh):
    return jax.shard_map(
        body,
        mesh=mesh,
        in_specs=(
            P("ex", None, "param"),
            P("ex", None, None),
            P("ex", None),
            P(None, "param"),
            P(),
        ),
        out_specs=(P("ex", "param"), P("ex", None)),
        check_vma=False,
    )
```

time: 1110 us -> 382 us (0.34)
  local copies, waits for them, and re-layouts: 539 us -> 1.73 us
  waiting for transfers between devices: 385 us -> 170 us
  matrix products: 153 us -> 4.52 us
  Pallas kernels: 0 us -> 128 us
  blocking collectives: 0 us -> 53.4 us
    gather x1 -> x0, local copies, waits for them, and re-layouts: 473 us -> none  [body(): jnp.take(local_values.reshape(count_ex, -1), position, axis=1)]
    all_gather x1 -> x0, waiting for transfers between devices: 227 us -> none  [body(): lax.all_gather(features, 'ex', axis=0, tiled=True)]
    dot_general x5 -> x1, matrix products: 153 us -> 4.52 us  [body(): lax.dot_general(swapped, swapped, (((1,), (1,)), ((), ())), precision=lax...]
    pallas_call x0 -> x2, Pallas kernels: none -> 128 us  [the longest x1 73.1 us: pick_features(): pl.pallas_call(functools.partial(pick_kernel, steps), grid_spec=pltpu.Pre...]
    reduce_scatter x0 -> x1, waiting for transfers between devices: none -> 62.4 us  [body(): tile_block = lax.psum_scatter(tile, 'ex', scatter_dimension=0, tiled=True)]
    reduce_scatter x1, waiting for transfers between devices: 128 us -> 74.2 us  [body(): lax.psum_scatter(partial_term, 'param', scatter_dimension=1, tiled=True)]
    all_to_all x0 -> x1, blocking collectives: none -> 53.4 us  [body(): lax.all_to_all(features, 'ex', split_axis=1, concat_axis=0, tiled=True)]
    another operation x1 -> x0, local copies, waits for them, and re-layouts: 45 us -> none  [body(): local_values.reshape(count_ex, -1)]
where the time goes in v1:
time: 382 us; the launch traced here: 381 us
  waiting for transfers between devices  170 us (45%)
  Pallas kernels  128 us (34%)
  blocking collectives  53.4 us (14%)
  between operations  13.8 us (4%)
  other arithmetic  9.61 us (3%)
  matrix products  4.52 us (1%)
    reduce_scatter x1, waiting for transfers between devices, body(): lax.psum_scatter(partial_term, 'param', scatter_dimension=1, tiled=True)  74.2 us
    pallas_call x1, Pallas kernels, pick_features(): pl.pallas_call(functools.partial(pick_kernel, steps), grid_spec=pltpu.Pre...  73.1 us
    reduce_scatter x1, waiting for transfers between devices, body(): tile_block = lax.psum_scatter(tile, 'ex', scatter_dimension=0, tiled=True)  62.4 us
    pallas_call x1, Pallas kernels, mix_rows(): pl.pallas_call(mix_kernel, grid=(width // block, count_ex // GROUP), in_s...  55.4 us
    all_to_all x1, blocking collectives, body(): lax.all_to_all(features, 'ex', split_axis=1, concat_axis=0, tiled=True)  53.4 us
    psum x1, waiting for transfers between devices, body(): gram = lax.psum(tile_block, 'param') / select.shape[0]  33.1 us
  transfers between devices with their start and end apart: 3, of which 3 were waited for; matrix products, arithmetic and copies ran while one was open for 0% of the time, Pallas kernels for 0%

profile of v1, /device:TPU:0, one launch (start us, length us, event | category | flops | bytes accessed | tf_op | source)
XLA Modules:
  0.0 381.2 jit_solution(7807032916375251155)
XLA Ops:
  7.2 0.0 reduce-scatter.3.cloned.1.call-start
  7.3 0.1 convert_convert_fusion
  7.3 0.8 broadcast_compare_fusion
  8.1 0.7 pad_maximum_fusion.1.table_ref
  8.8 0.6 pad_maximum_fusion.table_ref
  9.4 1.9 fusion.2
  11.3 1.7 convert_multiply_fusion
  13.0 2.3 select_bitcast_fusion.cots_ref
  15.3 55.4 %shard_map.68 = f32[64,64,2048]{2,1,0:T(8,128)} custom-call(bf16[64,64,128]{2,1,0:T(8,128)(2,1)} %select_bitcast_fusion.cots_ref, bf16[64,128,2048]{2,1,0:T(8,128)(2,1)} %acts_ref.1, s32[64,2048]{1,0:T(8,128)} %signs_ref.1, bf16[64,128]{1,0:T(8,128)(2,1)} %pad_maximum_fusion.1.table_ref), custom_call_target="tpu_custom_call" | custom-call | tf_op jit(solution)/shard_map/pallas_call | solution.py:53
  70.6 73.1 %shard_map.69 = f32[64,32768]{1,0:T(8,128)} custom-call(s32[32768]{0:T(1024)} %get-tuple-element.3.rows_ref, f32[2,32,64,2048]{3,2,1,0:T(8,128)} %bitcast.14, bf16[128,256]{1,0:T(8,128)(2,1)} %pad_maximum_fusion.table_ref, f32[1,32768]{1,0:T(1,128)} %bitcast.18, f32[1,32768]{1,0:T(1,128)} %bitcast.19), custom_call_target="tpu_custom_call" | custom-call | tf_op jit(solution)/shard_map/pallas_call | solution.py:124
  143.7 0.0 reduce-scatter.3.cloned.1.call-update
  143.7 0.0 reduce-scatter.5.cloned.1.call-start
  143.8 74.2 %reduce-scatter.3.cloned.1.call-done = f32[64,8192]{1,0:T(8,128)} async-done(((f32[64,32768]{1,0:T(8,128)}), f32[64,8192]{1,0:T(8,128)}) %reduce-scatter.3.cloned.1.call-update) | async-done | bytes 2097168 | tf_op jit(solution)/shard_map/reduce_scatter | solution.py:175
  218.0 1.7 copy.10
  219.7 53.4 %all_to_all.19 = f32[64,8,1024]{2,0,1:T(8,128)S(1)} all-to-all(f32[64,8,1024]{2,0,1:T(8,128)S(1)} %bitcast.16), channel_id=1, replica_groups=mesh['param'=4,'ex'=8] {'ex'}, dimensions={1} | all-to-all | bytes 4194304 | tf_op jit(solution)/shard_map/all_to_all | solution.py:176
  273.1 4.5 %fusion.10 = f32[512,512]{1,0:T(8,128)} fusion(f32[512,1024]{1,0:T(8,128)S(1)} %bitcast.15), kind=kOutput, calls=%fused_computation.37 | convolution fusion | flops 3221225472 | bytes 3145728 | tf_op jit(solution)/shard_map/dot_general | solution.py:177
  277.6 0.0 reduce-scatter.5.cloned.1.call-update
  277.6 0.0 all-reduce.2.cloned.1.call-start
  277.7 62.4 %reduce-scatter.5.cloned.1.call-done = f32[64,512]{1,0:T(8,128)} async-done(((f32[512,512]{1,0:T(8,128)}), f32[64,512]{1,0:T(8,128)}) %reduce-scatter.5.cloned.1.call-update) | async-done | bytes 131088 | tf_op jit(solution)/shard_map/reduce_scatter | solution.py:180
  340.1 0.0 all-reduce.2.cloned.1.call-update
  340.1 33.1 %all-reduce.2.cloned.1.call-done = f32[64,512]{1,0:T(8,128)} async-done(((f32[64,512]{1,0:T(8,128)}), f32[64,512]{1,0:T(8,128)}) %all-reduce.2.cloned.1.call-update) | async-done | bytes 131088 | tf_op jit(solution)/shard_map/psum | solution.py:181
  373.1 1.6 broadcast_multiply_fusion
  (1 shorter events, 0.0 us)
Async XLA Ops:
  7.2 210.8 %reduce-scatter.3.cloned.1.call-start = ((), (), s32[]{:S(2)}) async-start(), calls=%async_computation.3 | async-start | bytes 10485760 | tf_op jit(solution)/shard_map/reduce_scatter | solution.py:175
  143.7 196.3 %reduce-scatter.5.cloned.1.call-start = ((), (), s32[]{:S(2)}) async-start(), calls=%async_computation.4 | async-start | bytes 1179648 | tf_op jit(solution)/shard_map/reduce_scatter | solution.py:180
  277.6 95.5 %all-reduce.2.cloned.1.call-start = ((), (), s32[]{:S(2)}) async-start(), calls=%async_computation.5 | async-start | bytes 262144 | tf_op jit(solution)/shard_map/psum | solution.py:181
Sparse Core Ops, SparseCore 0:
  143.9 74.1 reduce-scatter.2
  277.8 62.2 reduce-scatter.4
  342.4 30.7 all-reduce.1

commit v2 on v1

--- a/solution.py
+++ b/solution.py
@@ -144,6 +144,91 @@
     )(rows, halves, table, upper, weight)
 
 
+def gram_kernel(sections, groups, count, tile_ref, out_ref, first, total, second, done, third, s1, r1, s2, r2, s3, r3):
+    mine, place = lax.axis_index("param"), lax.axis_index("ex")
+    height, width = out_ref.shape[0], total.shape[1]
+    barrier = pltpu.get_barrier_semaphore()
+    for d in range(1, sections):
+        pl.semaphore_signal(
+            barrier, inc=1, device_id={"param": lax.rem(mine + d, sections)}, device_id_type=pl.DeviceIdType.MESH
+        )
+    for d in range(1, groups):
+        pl.semaphore_signal(
+            barrier, inc=1, device_id={"ex": lax.rem(place + d, groups)}, device_id_type=pl.DeviceIdType.MESH
+        )
+    pl.semaphore_wait(barrier, sections + groups - 2)
+
+    def send(axis, target, source, landing, send_sem, recv_sem, d):
+        copy = pltpu.make_async_remote_copy(
+            src_ref=source,
+            dst_ref=landing.at[d - 1],
+            send_sem=send_sem.at[d - 1],
+            recv_sem=recv_sem.at[d - 1],
+            device_id={axis: target},
+            device_id_type=pl.DeviceIdType.MESH,
+        )
+        copy.start()
+        return copy
+
+    def columns(index):
+        return pl.ds(pl.multiple_of(index * width, width), width)
+
+    def lines(index):
+        return pl.ds(pl.multiple_of(index * height, height), height)
+
+    copies = []
+    for d in range(1, sections):
+        target = lax.rem(mine + d, sections)
+        copies.append(send("param", target, tile_ref.at[:, columns(target)], first, s1, r1, d))
+    total[...] = tile_ref[:, columns(mine)]
+    for d, copy in enumerate(copies):
+        copy.wait()
+        total[...] += first[d]
+    copies = []
+    for d in range(1, groups):
+        target = lax.rem(place + d, groups)
+        copies.append(send("ex", target, total.at[lines(target), :], second, s2, r2, d))
+    result = total[lines(place), :]
+    for d, copy in enumerate(copies):
+        copy.wait()
+        result = result + second[d]
+    done[...] = result / count
+    copies = []
+    for d in range(1, sections):
+        copies.append(send("param", lax.rem(mine + d, sections), done, third, s3, r3, d))
+    out_ref[:, columns(mine)] = done[...]
+    for d, copy in enumerate(copies):
+        copy.wait()
+        out_ref[:, columns(lax.rem(mine + sections - d - 1, sections))] = third[d]
+
+
+def reduce_gram(tile, count):
+    sections, groups = lax.axis_size("param"), lax.axis_size("ex")
+    examples = tile.shape[0]
+    height, width = examples // groups, examples // sections
+    dma = pltpu.SemaphoreType.DMA
+    return pl.pallas_call(
+        functools.partial(gram_kernel, sections, groups, count),
+        out_shape=jax.ShapeDtypeStruct((height, examples), jnp.float32),
+        in_specs=[pl.BlockSpec(memory_space=pltpu.VMEM)],
+        out_specs=pl.BlockSpec(memory_space=pltpu.VMEM),
+        scratch_shapes=[
+            pltpu.VMEM((sections - 1, examples, width), jnp.float32),
+            pltpu.VMEM((examples, width), jnp.float32),
+            pltpu.VMEM((groups - 1, height, width), jnp.float32),
+            pltpu.VMEM((height, width), jnp.float32),
+            pltpu.VMEM((sections - 1, height, width), jnp.float32),
+            dma((sections - 1,)),
+            dma((sections - 1,)),
+            dma((groups - 1,)),
+            dma((groups - 1,)),
+            dma((sections - 1,)),
+            dma((sections - 1,)),
+        ],
+        compiler_params=pltpu.CompilerParams(collective_id=1, has_side_effects=True),
+    )(tile)
+
+
 def body(activations, cotangents, token_ids, signs, select):
     local_width = activations.shape[2]
     toks = activations.shape[1]
@@ -177,8 +262,7 @@
     tile = lax.dot_general(
         swapped, swapped, (((1,), (1,)), ((), ())), precision=lax.Precision.HIGHEST
     )
-    tile_block = lax.psum_scatter(tile, "ex", scatter_dimension=0, tiled=True)
-    gram = lax.psum(tile_block, "param") / select.shape[0]
+    gram = reduce_gram(tile, select.shape[0])
     return (features, gram)
 
 

time: 382 us -> 311 us (0.81)
  waiting for transfers between devices: 170 us -> 74.3 us
  Pallas kernels: 128 us -> 152 us
    reduce_scatter x1 -> x0, waiting for transfers between devices: 62.4 us -> none  [body(): tile_block = lax.psum_scatter(tile, 'ex', scatter_dimension=0, tiled=True)]
    psum x1 -> x0, waiting for transfers between devices: 33.1 us -> none  [body(): gram = lax.psum(tile_block, 'param') / select.shape[0]]
    pallas_call x0 -> x1, Pallas kernels: none -> 23.7 us  [reduce_gram(): pl.pallas_call(functools.partial(gram_kernel, sections, groups, count), o...]
  transfers between devices with their start and end apart: 3 -> 1, of which waited for: 3 -> 1; matrix products, arithmetic and copies ran while one was open for 0% -> 0% of each run, Pallas kernels for 0% -> 0%
where the time goes in v2:
time: 311 us; the launch traced here: 310 us
  Pallas kernels  152 us (49%)
  waiting for transfers between devices  74.3 us (24%)
  blocking collectives  53.4 us (17%)
  between operations  14.1 us (5%)
  other arithmetic  8.05 us (3%)
  matrix products  4.52 us (1%)
  local copies, waits for them, and re-layouts  3.29 us (1%)
    reduce_scatter x1, waiting for transfers between devices, body(): lax.psum_scatter(partial_term, 'param', scatter_dimension=1, tiled=True)  74.3 us
    pallas_call x1, Pallas kernels, pick_features(): pl.pallas_call(functools.partial(pick_kernel, steps), grid_spec=pltpu.Pre...  73.1 us
    pallas_call x1, Pallas kernels, mix_rows(): pl.pallas_call(mix_kernel, grid=(width // block, count_ex // GROUP), in_s...  55.4 us
    all_to_all x1, blocking collectives, body(): lax.all_to_all(features, 'ex', split_axis=1, concat_axis=0, tiled=True)  53.4 us
    pallas_call x1, Pallas kernels, reduce_gram(): pl.pallas_call(functools.partial(gram_kernel, sections, groups, count), o...  23.7 us
  transfers between devices with their start and end apart: 1, of which 1 were waited for; matrix products, arithmetic and copies ran while one was open for 0% of the time, Pallas kernels for 0%

profile of v2, /device:TPU:0, one launch (start us, length us, event | category | flops | bytes accessed | tf_op | source)
XLA Modules:
  0.0 309.7 jit_solution(15263531401695937309)
XLA Ops:
  7.2 0.0 reduce-scatter.2.cloned.1.call-start
  7.3 0.1 convert_convert_fusion
  7.3 0.8 broadcast_compare_fusion
  8.1 0.7 pad_maximum_fusion.1.table_ref
  8.8 0.6 pad_maximum_fusion.table_ref
  9.4 1.9 fusion.2
  11.3 1.7 convert_multiply_fusion
  13.0 2.3 select_bitcast_fusion.cots_ref
  15.3 55.4 %shard_map.68 = f32[64,64,2048]{2,1,0:T(8,128)} custom-call(bf16[64,64,128]{2,1,0:T(8,128)(2,1)} %select_bitcast_fusion.cots_ref, bf16[64,128,2048]{2,1,0:T(8,128)(2,1)} %acts_ref.1, s32[64,2048]{1,0:T(8,128)} %signs_ref.1, bf16[64,128]{1,0:T(8,128)(2,1)} %pad_maximum_fusion.1.table_ref), custom_call_target="tpu_custom_call" | custom-call | tf_op jit(solution)/shard_map/pallas_call | solution.py:53
  70.6 73.1 %shard_map.69 = f32[64,32768]{1,0:T(8,128)} custom-call(s32[32768]{0:T(1024)} %get-tuple-element.3.rows_ref, f32[2,32,64,2048]{3,2,1,0:T(8,128)} %bitcast.14, bf16[128,256]{1,0:T(8,128)(2,1)} %pad_maximum_fusion.table_ref, f32[1,32768]{1,0:T(1,128)} %bitcast.18, f32[1,32768]{1,0:T(1,128)} %bitcast.19), custom_call_target="tpu_custom_call" | custom-call | tf_op jit(solution)/shard_map/pallas_call | solution.py:124
  143.7 0.0 reduce-scatter.2.cloned.1.call-update
  143.7 74.3 %reduce-scatter.2.cloned.1.call-done = f32[64,8192]{1,0:T(8,128)} async-done(((f32[64,32768]{1,0:T(8,128)}), f32[64,8192]{1,0:T(8,128)}) %reduce-scatter.2.cloned.1.call-update) | async-done | bytes 2097168 | tf_op jit(solution)/shard_map/reduce_scatter | solution.py:260
  218.0 1.7 copy.10
  219.7 53.4 %all_to_all.19 = f32[64,8,1024]{2,0,1:T(8,128)S(1)} all-to-all(f32[64,8,1024]{2,0,1:T(8,128)S(1)} %bitcast.16), channel_id=1, replica_groups=mesh['param'=4,'ex'=8] {'ex'}, dimensions={1} | all-to-all | bytes 4194304 | tf_op jit(solution)/shard_map/all_to_all | solution.py:261
  273.1 4.5 %fusion.10.tile_ref = f32[512,512]{1,0:T(8,128)} fusion(f32[512,1024]{1,0:T(8,128)S(1)} %bitcast.15), kind=kOutput, calls=%fused_computation.36 | convolution fusion | flops 3221225472 | bytes 3145728 | tf_op jit(solution)/shard_map/dot_general | solution.py:262
  277.6 23.7 %shard_map.70 = f32[64,512]{1,0:T(8,128)} custom-call(f32[512,512]{1,0:T(8,128)} %fusion.10.tile_ref), custom_call_target="tpu_custom_call" | custom-call | tf_op jit(solution)/shard_map/pallas_call | solution.py:210
  301.3 1.6 copy.12
  (1 shorter events, 0.0 us)
Async XLA Ops:
  7.2 210.8 %reduce-scatter.2.cloned.1.call-start = ((), (), s32[]{:S(2)}) async-start(), calls=%async_computation.2 | async-start | bytes 10485760 | tf_op jit(solution)/shard_map/reduce_scatter | solution.py:260
Sparse Core Ops, SparseCore 0:
  143.9 74.1 reduce-scatter.1

commit v3 on v2

--- a/solution.py
+++ b/solution.py
@@ -142,6 +142,135 @@
         out_shape=jax.ShapeDtypeStruct((count_ex, count), jnp.float32),
         compiler_params=pltpu.CompilerParams(vmem_limit_bytes=60 * 1024 * 1024),
     )(rows, halves, table, upper, weight)
+
+
+def share_kernel(
+    rows_of_y, groups, part_ref, out_ref, tile_ref, near, sums, far, whole, near_s, near_r, far_s, far_r, ex_s, ex_r
+):
+    mine, place = lax.axis_index("param"), lax.axis_index("ex")
+    my_y, my_core = mine // 2, lax.rem(mine, 2)
+    height, block = out_ref.shape
+    width = block // groups
+    barrier = pltpu.get_barrier_semaphore()
+    mesh_type = pl.DeviceIdType.MESH
+
+    def owner(dy, core):
+        return lax.rem(my_y + dy, rows_of_y) * 2 + core
+
+    pl.semaphore_signal(barrier, inc=1, device_id={"param": owner(0, 1 - my_core)}, device_id_type=mesh_type)
+    for dy in range(1, rows_of_y):
+        pl.semaphore_signal(barrier, inc=1, device_id={"param": owner(dy, my_core)}, device_id_type=mesh_type)
+    for d in range(1, groups):
+        pl.semaphore_signal(
+            barrier, inc=1, device_id={"ex": lax.rem(place + d, groups)}, device_id_type=mesh_type
+        )
+    pl.semaphore_wait(barrier, rows_of_y + groups - 1)
+
+    def part(dy, core, slot):
+        start = owner(dy, core) * block + slot * width
+        return (slice(None), pl.ds(pl.multiple_of(start, width), width))
+
+    def send(target, source, landing, send_sem, recv_sem):
+        copy = pltpu.make_async_remote_copy(
+            src_ref=source,
+            dst_ref=landing,
+            send_sem=send_sem,
+            recv_sem=recv_sem,
+            device_id=target,
+            device_id_type=mesh_type,
+        )
+        copy.start()
+        return copy
+
+    order = list(range(1, groups)) + [0]
+    slots = {m: lax.rem(place + m, groups) for m in order}
+    offsets = list(range(1, rows_of_y)) + [0]
+    near_copies, far_copies, ex_copies = {}, {}, {}
+    for m in order:
+        for dy in offsets:
+            n = m * rows_of_y + dy
+            near_copies[m, dy] = send(
+                {"param": owner(0, 1 - my_core)},
+                part_ref.at[part(dy, 1 - my_core, slots[m])],
+                near.at[n],
+                near_s.at[n],
+                near_r.at[n],
+            )
+    for m in order:
+        for dy in offsets:
+            near_copies[m, dy].wait_recv()
+            joined = part_ref[part(dy, my_core, slots[m])] + near[m * rows_of_y + dy]
+            if dy == 0:
+                out_ref[:, pl.ds(pl.multiple_of(slots[m] * width, width), width)] = joined
+            else:
+                n = m * (rows_of_y - 1) + dy - 1
+                sums[n] = joined
+                far_copies[m, dy] = send(
+                    {"param": owner(dy, my_core)}, sums.at[n], far.at[n], far_s.at[n], far_r.at[n]
+                )
+    my_lines = pl.ds(pl.multiple_of(place * height, height), height)
+    for m in order:
+        here = pl.ds(pl.multiple_of(slots[m] * width, width), width)
+        joined = out_ref[:, here]
+        for dy in range(1, rows_of_y):
+            far_copies[m, dy].wait_recv()
+            joined = joined + far[m * (rows_of_y - 1) + dy - 1]
+        out_ref[:, here] = joined
+        if m == 0:
+            whole[my_lines, :] = joined
+        else:
+            ex_copies[m] = send(
+                {"ex": slots[m]}, out_ref.at[:, here], whole.at[my_lines, :], ex_s.at[m], ex_r.at[m]
+            )
+    for copy in near_copies.values():
+        copy.wait_send()
+    for copy in far_copies.values():
+        copy.wait_send()
+    for copy in ex_copies.values():
+        copy.wait()
+    tile_ref[...] = lax.dot_general(
+        whole[...],
+        whole[...],
+        (((1,), (1,)), ((), ())),
+        precision=lax.Precision.HIGHEST,
+        preferred_element_type=jnp.float32,
+    )
+
+
+def share_features(partial_term):
+    sections, groups = lax.axis_size("param"), lax.axis_size("ex")
+    height, count = partial_term.shape
+    rows_of_y = sections // 2
+    block = count // sections
+    width = block // groups
+    examples = height * groups
+    dma = pltpu.SemaphoreType.DMA
+    near_count, far_count = groups * rows_of_y, groups * max(rows_of_y - 1, 1)
+    vmem = pl.BlockSpec(memory_space=pltpu.VMEM)
+    return pl.pallas_call(
+        functools.partial(share_kernel, rows_of_y, groups),
+        out_shape=(
+            jax.ShapeDtypeStruct((height, block), jnp.float32),
+            jax.ShapeDtypeStruct((examples, examples), jnp.float32),
+        ),
+        in_specs=[vmem],
+        out_specs=(vmem, vmem),
+        scratch_shapes=[
+            pltpu.VMEM((near_count, height, width), jnp.float32),
+            pltpu.VMEM((far_count, height, width), jnp.float32),
+            pltpu.VMEM((far_count, height, width), jnp.float32),
+            pltpu.VMEM((examples, width), jnp.float32),
+            dma((near_count,)),
+            dma((near_count,)),
+            dma((far_count,)),
+            dma((far_count,)),
+            dma((groups,)),
+            dma((groups,)),
+        ],
+        compiler_params=pltpu.CompilerParams(
+            collective_id=2, has_side_effects=True, vmem_limit_bytes=60 * 1024 * 1024
+        ),
+    )(partial_term)
 
 
 def gram_kernel(sections, groups, count, tile_ref, out_ref, first, total, second, done, third, s1, r1, s2, r2, s3, r3):
@@ -257,11 +386,7 @@
     partial_term = pick_features(
         rows, mixed, jnp.concatenate([lane_table, lane_table], axis=1), upper[None, :], weight[None, :]
     )
-    features = lax.psum_scatter(partial_term, "param", scatter_dimension=1, tiled=True)
-    swapped = lax.all_to_all(features, "ex", split_axis=1, concat_axis=0, tiled=True)
-    tile = lax.dot_general(
-        swapped, swapped, (((1,), (1,)), ((), ())), precision=lax.Precision.HIGHEST
-    )
+    features, tile = share_features(partial_term)
     gram = reduce_gram(tile, select.shape[0])
     return (features, gram)
 

time: 311 us -> 244 us (0.78)
  Pallas kernels: 152 us -> 229 us
  waiting for transfers between devices: 74.3 us -> 0 us
  blocking collectives: 53.4 us -> 0 us
  between operations: 14.1 us -> 0.66 us
  matrix products: 4.52 us -> 0 us
    reduce_scatter x1 -> x0, waiting for transfers between devices: 74.3 us -> none  [body(): lax.psum_scatter(partial_term, 'param', scatter_dimension=1, tiled=True)]
    pallas_call x0 -> x1, Pallas kernels: none -> 70.4 us  [share_features(): pl.pallas_call(functools.partial(share_kernel, rows_of_y, groups), out_sh...]
    all_to_all x1 -> x0, blocking collectives: 53.4 us -> none  [body(): lax.all_to_all(features, 'ex', split_axis=1, concat_axis=0, tiled=True)]
    pallas_call x1, Pallas kernels: 23.7 us -> 30.6 us  [reduce_gram(): pl.pallas_call(functools.partial(gram_kernel, sections, groups, count), o...]
    dot_general x1 -> x0, matrix products: 4.52 us -> none  [body(): lax.dot_general(swapped, swapped, (((1,), (1,)), ((), ())), precision=lax...]
  transfers between devices with their start and end apart: 1 -> 0, of which waited for: 1 -> 0; matrix products, arithmetic and copies ran while one was open for 0% -> 0% of each run, Pallas kernels for 0% -> 0%
where the time goes in v3:
time: 244 us; the launch traced here: 243 us
  Pallas kernels  229 us (94%)
  other arithmetic  8.05 us (3%)
  local copies, waits for them, and re-layouts  4.63 us (2%)
    pallas_call x1, Pallas kernels, pick_features(): pl.pallas_call(functools.partial(pick_kernel, steps), grid_spec=pltpu.Pre...  73.1 us
    pallas_call x1, Pallas kernels, share_features(): pl.pallas_call(functools.partial(share_kernel, rows_of_y, groups), out_sh...  70.4 us
    pallas_call x1, Pallas kernels, mix_rows(): pl.pallas_call(mix_kernel, grid=(width // block, count_ex // GROUP), in_s...  55.4 us
    pallas_call x1, Pallas kernels, reduce_gram(): pl.pallas_call(functools.partial(gram_kernel, sections, groups, count), o...  30.6 us

profile of v3, /device:TPU:0, one launch (start us, length us, event | category | flops | bytes accessed | tf_op | source)
XLA Modules:
  0.0 242.8 jit_solution(12548454702013716474)
XLA Ops:
  0.6 0.8 broadcast_compare_fusion
  1.4 0.7 pad_maximum_fusion.1.table_ref
  2.1 0.1 convert_convert_fusion
  2.2 0.6 pad_maximum_fusion.table_ref
  2.8 1.7 convert_multiply_fusion
  4.5 1.9 fusion.2
  6.4 2.3 select_bitcast_fusion.cots_ref
  8.7 55.4 %shard_map.68 = f32[64,64,2048]{2,1,0:T(8,128)} custom-call(bf16[64,64,128]{2,1,0:T(8,128)(2,1)} %select_bitcast_fusion.cots_ref, bf16[64,128,2048]{2,1,0:T(8,128)(2,1)} %acts_ref.1, s32[64,2048]{1,0:T(8,128)} %signs_ref.1, bf16[64,128]{1,0:T(8,128)(2,1)} %pad_maximum_fusion.1.table_ref), custom_call_target="tpu_custom_call" | custom-call | tf_op jit(solution)/shard_map/pallas_call | solution.py:53
  64.1 73.1 %shard_map.69.part_ref = f32[64,32768]{1,0:T(8,128)} custom-call(s32[32768]{0:T(1024)} %get-tuple-element.7.rows_ref, f32[2,32,64,2048]{3,2,1,0:T(8,128)} %bitcast.5, bf16[128,256]{1,0:T(8,128)(2,1)} %pad_maximum_fusion.table_ref, f32[1,32768]{1,0:T(1,128)} %bitcast.6, f32[1,32768]{1,0:T(1,128)} %bitcast.7), custom_call_target="tpu_custom_call" | custom-call | tf_op jit(solution)/shard_map/pallas_call | solution.py:124
  137.2 70.4 %shard_map.70 = (f32[64,8192]{1,0:T(8,128)}, f32[512,512]{1,0:T(8,128)}) custom-call(f32[64,32768]{1,0:T(8,128)} %shard_map.69.part_ref), custom_call_target="tpu_custom_call" | custom-call | tf_op jit(solution)/shard_map/pallas_call | solution.py:250
  207.6 30.6 %shard_map.71 = f32[64,512]{1,0:T(8,128)} custom-call(f32[512,512]{1,0:T(8,128)} %get-tuple-element.5.tile_ref), custom_call_target="tpu_custom_call" | custom-call | tf_op jit(solution)/shard_map/pallas_call | solution.py:339
  238.2 3.1 %copy.9 = f32[64,8192]{1,0:T(8,128)} copy(f32[64,8192]{1,0:T(8,128)} %get-tuple-element.10) | data formatting | bytes 4194304
  241.3 1.6 copy.10
  (1 shorter events, 0.0 us)

commit v4 on v3

--- a/solution.py
+++ b/solution.py
@@ -27,42 +27,63 @@
     return high, low
 
 
-def mix_kernel(cots_ref, acts_ref, signs_ref, table_ref, out_ref, held):
-    slab_rows = out_ref.shape[0]
-    blocks = out_ref.shape[2] // LANES
-    flip = signs_ref[...].astype(jnp.float32)
-    for e in range(GROUP):
-        gradient = jnp.dot(cots_ref[e], acts_ref[e], preferred_element_type=jnp.float32)
-        high, low = split_two(gradient * flip)
-        mixed = jnp.dot(
-            table_ref[...], jnp.concatenate([high, low], axis=0), preferred_element_type=jnp.float32
-        )
-        for c in range(blocks):
-            held[pl.ds((c * GROUP + e) * slab_rows, slab_rows), :] = mixed[:, c * LANES:(c + 1) * LANES]
-    for r in range(slab_rows):
-        for c in range(blocks):
-            out_ref[r, :, c * LANES:(c + 1) * LANES] = held[
-                pl.ds(c * GROUP * slab_rows + r, GROUP, stride=slab_rows), :
-            ]
-
-
-def mix_rows(cots, acts, signs, table):
-    count_ex, slab_rows, toks = cots.shape
+def butterfly(part):
+    span = 1
+    while span < len(part):
+        part = [
+            part[a] + part[a + span] if a & span == 0 else part[a - span] - part[a] for a in range(len(part))
+        ]
+        span *= 2
+    return part
+
+
+def mix_kernel(cots_ref, acts_ref, signs_ref, apart_ref, out_ref, held):
+    slab_rows, group, block = out_ref.shape
+    toks = cots_ref.shape[2]
+    spread = jnp.concatenate([cots_ref[0]] * group, axis=1) * apart_ref[...]
+    held[...] = jnp.dot(
+        spread, acts_ref[...].reshape(group * toks, block), preferred_element_type=jnp.float32
+    )
+    radix = 8
+    for c in range(block // LANES):
+        lanes = slice(c * LANES, (c + 1) * LANES)
+        flip = signs_ref[:, lanes].astype(jnp.float32)
+        for high in range(slab_rows // radix):
+            rows = [high * radix + j for j in range(radix)]
+            part = butterfly([
+                held[r * group:(r + 1) * group, lanes] * jnp.broadcast_to(flip[r:r + 1], (group, LANES))
+                for r in rows
+            ])
+            for r, value in zip(rows, part):
+                held[r * group:(r + 1) * group, lanes] = value
+        for low in range(radix):
+            rows = list(range(low, slab_rows, radix))
+            part = butterfly([held[r * group:(r + 1) * group, lanes] for r in rows])
+            for r, value in zip(rows, part):
+                out_ref[r, :, lanes] = value
+
+
+def mix_rows(cots, acts, signs):
+    count_ex, toks, slab_rows = cots.shape
     width = acts.shape[2]
     block = min(width, 1024)
+    spread = cots.reshape(count_ex // GROUP, GROUP, toks, slab_rows).transpose(0, 3, 1, 2)
+    spread = spread.reshape(count_ex // GROUP, slab_rows * GROUP, toks)
+    shape = (slab_rows * GROUP, GROUP * toks)
+    apart = lax.broadcasted_iota(jnp.int32, shape, 0) % GROUP == lax.broadcasted_iota(jnp.int32, shape, 1) // toks
     return pl.pallas_call(
         mix_kernel,
         grid=(width // block, count_ex // GROUP),
         in_specs=[
-            pl.BlockSpec((GROUP, slab_rows, toks), lambda c, e: (e, 0, 0)),
+            pl.BlockSpec((1, slab_rows * GROUP, toks), lambda c, e: (e, 0, 0)),
             pl.BlockSpec((GROUP, toks, block), lambda c, e: (e, 0, c)),
             pl.BlockSpec((slab_rows, block), lambda c, e: (0, c)),
-            pl.BlockSpec(table.shape, lambda c, e: (0, 0)),
+            pl.BlockSpec(shape, lambda c, e: (0, 0)),
         ],
         out_specs=pl.BlockSpec((slab_rows, GROUP, block), lambda c, e: (0, e, c)),
         out_shape=jax.ShapeDtypeStruct((slab_rows, count_ex, width), jnp.float32),
-        scratch_shapes=[pltpu.VMEM((GROUP * slab_rows * block // LANES, LANES), jnp.float32)],
-    )(cots, acts, signs, table)
+        scratch_shapes=[pltpu.VMEM((slab_rows * GROUP, block), jnp.float32)],
+    )(spread, acts, signs, apart.astype(jnp.bfloat16))
 
 
 def pick_kernel(steps, rows_ref, mixed_ref, table_ref, upper_ref, weight_ref, out_ref, values, pieces, picked):
@@ -366,11 +387,8 @@
     width = local_width * section_count
     live_mask = token_ids != 0
     masked = jnp.where(live_mask[:, :, None], cotangents, jnp.zeros((), cotangents.dtype))
-    row_table = walsh_table(slab_rows).astype(jnp.bfloat16)
     lane_table = walsh_table(LANES).astype(jnp.bfloat16)
-    mixed = mix_rows(
-        jnp.swapaxes(masked, 1, 2), activations, signs, jnp.concatenate([row_table, row_table], axis=1)
-    )
+    mixed = mix_rows(masked, activations, signs)
     factor = 1.0 / float(toks * slab_rows * width) ** 0.5
     my_index = lax.axis_index("param")
     column = select % width

time: 244 us -> 225 us (0.922)
  Pallas kernels: 229 us -> 211 us
    pallas_call x1, Pallas kernels: 55.4 us -> 37.2 us  [mix_rows(): pl.pallas_call(mix_kernel, grid=(width // block, count_ex // GROUP), in_s...]
where the time goes in v4:
time: 225 us; the launch traced here: 224 us
  Pallas kernels  211 us (94%)
  other arithmetic  6.5 us (3%)
  local copies, waits for them, and re-layouts  5.45 us (2%)
    pallas_call x1, Pallas kernels, pick_features(): pl.pallas_call(functools.partial(pick_kernel, steps), grid_spec=pltpu.Pre...  73.1 us
    pallas_call x1, Pallas kernels, share_features(): pl.pallas_call(functools.partial(share_kernel, rows_of_y, groups), out_sh...  70.4 us
    pallas_call x1, Pallas kernels, mix_rows(): pl.pallas_call(mix_kernel, grid=(width // block, count_ex // GROUP), in_s...  37.2 us
    pallas_call x1, Pallas kernels, reduce_gram(): pl.pallas_call(functools.partial(gram_kernel, sections, groups, count), o...  30.6 us

profile of v4, /device:TPU:0, one launch (start us, length us, event | category | flops | bytes accessed | tf_op | source)
XLA Modules:
  0.0 224.0 jit_solution(4776183032979863151)
XLA Ops:
  0.6 0.0 copy-start
  0.7 0.8 broadcast_compare_fusion
  1.5 0.1 convert_convert_fusion
  1.6 0.6 pad_maximum_fusion.table_ref
  2.2 1.7 convert_multiply_fusion
  3.9 1.9 fusion.3
  5.8 1.2 fusion.apart_ref
  7.1 0.0 copy-done
  7.1 0.1 broadcast_select_fusion
  7.2 1.7 copy.9
  8.9 37.2 %shard_map.68 = f32[64,64,2048]{2,1,0:T(8,128)} custom-call(bf16[8,512,128]{2,1,0:T(8,128)(2,1)} %bitcast.10, bf16[64,128,2048]{2,1,0:T(8,128)(2,1)} %acts_ref.1, s32[64,2048]{1,0:T(8,128)} %signs_ref.1, bf16[512,1024]{1,0:T(8,128)(2,1)} %fusion.apart_ref), custom_call_target="tpu_custom_call" | custom-call | tf_op jit(solution)/shard_map/pallas_call | solution.py:74
  46.1 73.1 %shard_map.69.part_ref = f32[64,32768]{1,0:T(8,128)} custom-call(s32[32768]{0:T(1024)} %get-tuple-element.7.rows_ref, f32[2,32,64,2048]{3,2,1,0:T(8,128)} %bitcast.9, bf16[128,256]{1,0:T(8,128)(2,1)} %pad_maximum_fusion.table_ref, f32[1,32768]{1,0:T(1,128)} %bitcast.12, f32[1,32768]{1,0:T(1,128)} %bitcast.13), custom_call_target="tpu_custom_call" | custom-call | tf_op jit(solution)/shard_map/pallas_call | solution.py:145
  119.2 70.4 %shard_map.70 = (f32[64,8192]{1,0:T(8,128)}, f32[512,512]{1,0:T(8,128)}) custom-call(f32[64,32768]{1,0:T(8,128)} %shard_map.69.part_ref), custom_call_target="tpu_custom_call" | custom-call | tf_op jit(solution)/shard_map/pallas_call | solution.py:271
  189.6 30.6 %shard_map.71 = f32[64,512]{1,0:T(8,128)} custom-call(f32[512,512]{1,0:T(8,128)} %get-tuple-element.5.tile_ref), custom_call_target="tpu_custom_call" | custom-call | tf_op jit(solution)/shard_map/pallas_call | solution.py:360
  220.2 0.0 copy-start.1
  220.2 3.1 %copy.12 = f32[64,8192]{1,0:T(8,128)} copy(f32[64,8192]{1,0:T(8,128)} %get-tuple-element.14) | data formatting | bytes 4194304
  223.3 0.0 copy-done.1
  223.3 0.7 copy.13
  (4 shorter events, 0.0 us)
Async XLA Ops:
  0.6 6.4 %copy-start = (bf16[64,128,64]{1,2,0:T(8,128)(2,1)S(1)}, bf16[64,128,64]{1,2,0:T(8,128)(2,1)}, u32[]{:S(2)}) copy-start(bf16[64,128,64]{1,2,0:T(8,128)(2,1)} %param.6) | copy-start | bytes 3145732
  220.2 3.1 %copy-start.1 = (f32[64,512]{1,0:T(8,128)S(1)}, f32[64,512]{1,0:T(8,128)}, u32[]{:S(2)}) copy-start(f32[64,512]{1,0:T(8,128)} %shard_map.71) | copy-start | bytes 393220

commit v5 on v4

--- a/solution.py
+++ b/solution.py
@@ -249,13 +249,12 @@
         copy.wait_send()
     for copy in ex_copies.values():
         copy.wait()
-    tile_ref[...] = lax.dot_general(
-        whole[...],
-        whole[...],
-        (((1,), (1,)), ((), ())),
-        precision=lax.Precision.HIGHEST,
-        preferred_element_type=jnp.float32,
-    )
+    high, low = split_two(whole[...])
+
+    def inner(left, right):
+        return lax.dot_general(left, right, (((1,), (1,)), ((), ())), preferred_element_type=jnp.float32)
+
+    tile_ref[...] = inner(high, low) + inner(low, high) + inner(high, high)
 
 
 def share_features(partial_term):
@@ -294,7 +293,10 @@
     )(partial_term)
 
 
-def gram_kernel(sections, groups, count, tile_ref, out_ref, first, total, second, done, third, s1, r1, s2, r2, s3, r3):
+def gram_kernel(
+    sections, groups, count, tile_ref, out_ref, near, sums, first, total, second, done, third,
+    s0, r0, s1, r1, s2, r2, s3, r3,
+):
     mine, place = lax.axis_index("param"), lax.axis_index("ex")
     height, width = out_ref.shape[0], total.shape[1]
     barrier = pltpu.get_barrier_semaphore()
@@ -326,11 +328,25 @@
     def lines(index):
         return pl.ds(pl.multiple_of(index * height, height), height)
 
-    copies = []
-    for d in range(1, sections):
-        target = lax.rem(mine + d, sections)
-        copies.append(send("param", target, tile_ref.at[:, columns(target)], first, s1, r1, d))
-    total[...] = tile_ref[:, columns(mine)]
+    rows_of_y = sections // 2
+    my_core = lax.rem(mine, 2)
+
+    def owner(dy, core):
+        return lax.rem(mine // 2 + dy, rows_of_y) * 2 + core
+
+    near_copies, copies = {}, []
+    offsets = list(range(1, rows_of_y)) + [0]
+    for dy in offsets:
+        source = tile_ref.at[:, columns(owner(dy, 1 - my_core))]
+        near_copies[dy] = send("param", owner(0, 1 - my_core), source, near, s0, r0, dy + 1)
+    for dy in offsets:
+        near_copies[dy].wait()
+        joined = tile_ref[:, columns(owner(dy, my_core))] + near[dy]
+        if dy == 0:
+            total[...] = joined
+        else:
+            sums[dy - 1] = joined
+            copies.append(send("param", owner(dy, my_core), sums.at[dy - 1], first, s1, r1, dy))
     for d, copy in enumerate(copies):
         copy.wait()
         total[...] += first[d]
@@ -363,13 +379,17 @@
         in_specs=[pl.BlockSpec(memory_space=pltpu.VMEM)],
         out_specs=pl.BlockSpec(memory_space=pltpu.VMEM),
         scratch_shapes=[
-            pltpu.VMEM((sections - 1, examples, width), jnp.float32),
+            pltpu.VMEM((sections // 2, examples, width), jnp.float32),
+            pltpu.VMEM((max(sections // 2 - 1, 1), examples, width), jnp.float32),
+            pltpu.VMEM((max(sections // 2 - 1, 1), examples, width), jnp.float32),
             pltpu.VMEM((examples, width), jnp.float32),
             pltpu.VMEM((groups - 1, height, width), jnp.float32),
             pltpu.VMEM((height, width), jnp.float32),
             pltpu.VMEM((sections - 1, height, width), jnp.float32),
-            dma((sections - 1,)),
-            dma((sections - 1,)),
+            dma((sections // 2,)),
+            dma((sections // 2,)),
+            dma((max(sections // 2 - 1, 1),)),
+            dma((max(sections // 2 - 1, 1),)),
             dma((groups - 1,)),
             dma((groups - 1,)),
             dma((sections - 1,)),

time: 225 us -> 222 us (0.987)
  Pallas kernels: 211 us -> 208 us
where the time goes in v5:
time: 222 us; the launch traced here: 220 us
  Pallas kernels  208 us (94%)
  other arithmetic  6.5 us (3%)
  local copies, waits for them, and re-layouts  5.45 us (2%)
    pallas_call x1, Pallas kernels, pick_features(): pl.pallas_call(functools.partial(pick_kernel, steps), grid_spec=pltpu.Pre...  73.1 us
    pallas_call x1, Pallas kernels, share_features(): pl.pallas_call(functools.partial(share_kernel, rows_of_y, groups), out_sh...  68.8 us
    pallas_call x1, Pallas kernels, mix_rows(): pl.pallas_call(mix_kernel, grid=(width // block, count_ex // GROUP), in_s...  37.2 us
    pallas_call x1, Pallas kernels, reduce_gram(): pl.pallas_call(functools.partial(gram_kernel, sections, groups, count), o...  28.7 us

profile of v5, /device:TPU:0, one launch (start us, length us, event | category | flops | bytes accessed | tf_op | source)
XLA Modules:
  0.0 220.4 jit_solution(18252664810469277254)
XLA Ops:
  0.6 0.0 copy-start
  0.7 0.8 broadcast_compare_fusion
  1.5 0.1 convert_convert_fusion
  1.6 0.6 pad_maximum_fusion.table_ref
  2.2 1.7 convert_multiply_fusion
  3.9 1.9 fusion.3
  5.8 1.2 fusion.apart_ref
  7.1 0.0 copy-done
  7.1 0.1 broadcast_select_fusion
  7.2 1.7 copy.9
  8.9 37.2 %shard_map.68 = f32[64,64,2048]{2,1,0:T(8,128)} custom-call(bf16[8,512,128]{2,1,0:T(8,128)(2,1)} %bitcast.10, bf16[64,128,2048]{2,1,0:T(8,128)(2,1)} %acts_ref.1, s32[64,2048]{1,0:T(8,128)} %signs_ref.1, bf16[512,1024]{1,0:T(8,128)(2,1)} %fusion.apart_ref), custom_call_target="tpu_custom_call" | custom-call | tf_op jit(solution)/shard_map/pallas_call | solution.py:74
  46.1 73.1 %shard_map.69.part_ref = f32[64,32768]{1,0:T(8,128)} custom-call(s32[32768]{0:T(1024)} %get-tuple-element.7.rows_ref, f32[2,32,64,2048]{3,2,1,0:T(8,128)} %bitcast.9, bf16[128,256]{1,0:T(8,128)(2,1)} %pad_maximum_fusion.table_ref, f32[1,32768]{1,0:T(1,128)} %bitcast.12, f32[1,32768]{1,0:T(1,128)} %bitcast.13), custom_call_target="tpu_custom_call" | custom-call | tf_op jit(solution)/shard_map/pallas_call | solution.py:145
  119.2 68.8 %shard_map.70 = (f32[64,8192]{1,0:T(8,128)}, f32[512,512]{1,0:T(8,128)}) custom-call(f32[64,32768]{1,0:T(8,128)} %shard_map.69.part_ref), custom_call_target="tpu_custom_call" | custom-call | tf_op jit(solution)/shard_map/pallas_call | solution.py:270
  188.0 28.7 %shard_map.71 = f32[64,512]{1,0:T(8,128)} custom-call(f32[512,512]{1,0:T(8,128)} %get-tuple-element.5.tile_ref), custom_call_target="tpu_custom_call" | custom-call | tf_op jit(solution)/shard_map/pallas_call | solution.py:376
  216.6 0.0 copy-start.1
  216.7 3.1 %copy.12 = f32[64,8192]{1,0:T(8,128)} copy(f32[64,8192]{1,0:T(8,128)} %get-tuple-element.14) | data formatting | bytes 4194304
  219.7 0.0 copy-done.1
  219.8 0.7 copy.13
  (4 shorter events, 0.0 us)
Async XLA Ops:
  0.6 6.4 %copy-start = (bf16[64,128,64]{1,2,0:T(8,128)(2,1)S(1)}, bf16[64,128,64]{1,2,0:T(8,128)(2,1)}, u32[]{:S(2)}) copy-start(bf16[64,128,64]{1,2,0:T(8,128)(2,1)} %param.6) | copy-start | bytes 3145732
  216.6 3.1 %copy-start.1 = (f32[64,512]{1,0:T(8,128)S(1)}, f32[64,512]{1,0:T(8,128)}, u32[]{:S(2)}) copy-start(f32[64,512]{1,0:T(8,128)} %shard_map.71) | copy-start | bytes 393220
